TPU v7x, 32 devices: a whole 2x2x4 slice. The times are simulated.
32 devices in a mesh: dom: 8 (over z, y), rows: 4 (over x, core).
Axes of the slice: x: 2, y: 2, z: 4, core: 2. Of those that a mesh axis runs over, the one named last changes fastest.
Arguments:
- fields: float32 [8, 3, 128, 4096], P('dom', None, 'rows'), may hold values from -6 to 6
- depth: float32 [128, 4096], P('rows'), may hold values from 1.5 to 6
- obs_index: int32 [256], replicated, may hold values from 0 to 524287, as said below
- obs_value: float32 [256], replicated, may hold values from -6 to 6
- obs_var: float32 [256], replicated, may hold values from 0.5 to 5
- parent_lookup: int32 [8], replicated, may hold values from 0 to 7, as said below
Outputs:
- log_weights: float32 [8], P('dom')
- posterior_members: float32 [8, 3, 128, 4096], P('dom', None, 'rows')
Inputs may be any that keep to these rules, and one draw needn't show every extreme that they name: `parent_lookup`: every value is the index of a particle; 0 and 7 each appear; values may repeat. `obs_index`: indices of grid cells, possibly repeated; the first and last cell each appear.
All inputs are finite; a program needn't handle non-finite values.
Results may differ from a plain program's by a relative error of at most 0.00003.
Values sent between devices are 32-bit elements; how exact they have to be, the bound alone decides.
No kernel may reach another device: no remote copies, remote signals or barrier semaphores. Data moves between devices by JAX's collectives and lax.ppermute only.
A program may use at most 64 MiB of HBM per device.

v0:
```python
import jax
import jax.numpy as jnp
from jax import lax
from jax.sharding import PartitionSpec as P

STEPS = 4


time_step = 0.5
coriolis = 0.2


def extended(cells, sides, width):
    for axis, dim in sides:
        count = lax.axis_size(axis)
        ends = count - 1
        head = lax.slice_in_dim(cells, 0, width, axis=dim)
        tail = lax.slice_in_dim(cells, cells.shape[dim] - width, cells.shape[dim], axis=dim)
        cells = jnp.concatenate(
            [
                lax.ppermute(tail, axis, [(i, (i + 1) % count) for i in range(ends)]),
                cells,
                lax.ppermute(head, axis, [((i + 1) % count, i) for i in range(ends)]),
            ],
            axis=dim,
        )
    return cells


def cols_diff(a):
    return 0.5 * (jnp.roll(a, -1, axis=-1) - jnp.roll(a, 1, axis=-1))


def flux_rows_diff(a):
    padded = extended(a, (("rows", 1),), 1)
    return 0.5 * (padded[:, 2:] - padded[:, :-2])


def height_rows_diff(a):
    padded = extended(a, (("rows", 1),), 1)
    return 0.5 * (padded[:, 2:] - padded[:, :-2])


def shards(fields, depth, obs_index, obs_value, obs_var, parent_lookup):
    free_elevation = fields[:, 0]
    zonal_current = fields[:, 1]
    meridional_current = fields[:, 2]
    depth_rows = depth[None]
    for step in range(STEPS):
        free_elevation = free_elevation - time_step * (
            cols_diff(depth_rows * zonal_current) + flux_rows_diff(depth_rows * meridional_current)
        )
        zonal_current = (
            zonal_current
            - time_step * cols_diff(free_elevation)
            + time_step * coriolis * meridional_current
        )
        meridional_current = (
            meridional_current
            - time_step * height_rows_diff(free_elevation)
            - time_step * coriolis * zonal_current
        )
    prior_members = jnp.stack([free_elevation, zonal_current, meridional_current], axis=1)
    slab_cells = free_elevation.shape[1] * free_elevation.shape[2]
    flat = free_elevation.reshape(free_elevation.shape[0], slab_cells)
    offset = obs_index - lax.axis_index("rows") * slab_cells
    inside = (offset >= 0) & (offset < slab_cells)
    values = jnp.take(flat, jnp.clip(offset, 0, slab_cells - 1), axis=1)
    misfit = jnp.where(inside[None, :], (obs_value[None, :] - values) ** 2 / obs_var[None, :], 0.0)
    loglik = lax.psum(-0.5 * jnp.sum(misfit, axis=1), "rows")
    local_peak = jnp.max(loglik)
    peak = lax.pmax(local_peak, "dom")
    total = lax.psum(jnp.sum(jnp.exp(loglik - peak)), "dom")
    log_weights = loglik - (peak + jnp.log(total))
    member_batches = lax.axis_size("dom")
    subregion_tiles = prior_members.reshape(prior_members.shape[0], member_batches, -1)
    received = lax.all_to_all(subregion_tiles, "dom", split_axis=1, concat_axis=0, tiled=True)
    picked = jnp.take(received, parent_lookup, axis=0)
    final_answer = lax.all_to_all(picked, "dom", split_axis=0, concat_axis=1, tiled=True)
    posterior_members = final_answer.reshape(prior_members.shape)
    return (log_weights, posterior_members)


def solution(mesh):
    in_specs = (P("dom", None, "rows", None), P("rows", None), P(), P(), P(), P())
    out_specs = (P("dom"), P("dom", None, "rows", None))
    return jax.shard_map(shards, mesh=mesh, in_specs=in_specs, out_specs=out_specs, check_vma=False)
```

profile of v0, /device:TPU:0, one launch (start us, length us, event | category | flops | bytes accessed | tf_op | source)
XLA Modules:
  0.0 196.9 jit_solution(10956344238698657955)
XLA Ops:
  0.6 1.5 fusion.51
  2.1 1.4 collective-permute-start
  3.6 3.0 %collective-permute-start.1 = (f32[1,1,4096]{2,1,0:T(1,128)S(1)}, f32[1,1,4096]{2,1,0:T(1,128)S(1)}, u32[]{:S(2)}, u32[]{:S(2)}) collective-permute-start(f32[1,1,4096]{2,1,0:T(1,128)S(1)} %get-tuple-element.68), channel_id=1, source_target_pairs={{0,1},{1,2},{2,3},{4,5},{5,6},{6,7},{8,9},{9,10},{10,11},{12,13},{... | collective-permute-start | bytes 49160 | tf_op jit(solution)/shard_map/ppermute | solution.py:21
  9.3 5.1 %collective-permute-start.3 = (f32[1,1,4096]{2,1,0:T(1,128)S(1)}, f32[1,1,4096]{2,1,0:T(1,128)S(1)}, u32[]{:S(2)}, u32[]{:S(2)}) collective-permute-start(f32[1,1,4096]{2,1,0:T(1,128)S(1)} %get-tuple-element.62), channel_id=1, source_target_pairs={{0,1},{1,2},{2,3},{4,5},{5,6},{6,7},{8,9},{9,10},{10,11},{12,13},{... | collective-permute-start | bytes 49160 | tf_op jit(solution)/shard_map/ppermute | solution.py:21
  17.0 4.9 %collective-permute-start.5 = (f32[1,1,4096]{2,1,0:T(1,128)S(1)}, f32[1,1,4096]{2,1,0:T(1,128)S(1)}, u32[]{:S(2)}, u32[]{:S(2)}) collective-permute-start(f32[1,1,4096]{2,1,0:T(1,128)S(1)} %get-tuple-element.60), channel_id=1, source_target_pairs={{0,1},{1,2},{2,3},{4,5},{5,6},{6,7},{8,9},{9,10},{10,11},{12,13},{... | collective-permute-start | bytes 49160 | tf_op jit(solution)/shard_map/ppermute | solution.py:21
  24.5 4.9 %collective-permute-start.7 = (f32[1,1,4096]{2,1,0:T(1,128)S(1)}, f32[1,1,4096]{2,1,0:T(1,128)S(1)}, u32[]{:S(2)}, u32[]{:S(2)}) collective-permute-start(f32[1,1,4096]{2,1,0:T(1,128)S(1)} %get-tuple-element.42), channel_id=1, source_target_pairs={{0,1},{1,2},{2,3},{4,5},{5,6},{6,7},{8,9},{9,10},{10,11},{12,13},{... | collective-permute-start | bytes 49160 | tf_op jit(solution)/shard_map/ppermute | solution.py:21
  31.7 4.9 %collective-permute-start.9 = (f32[1,1,4096]{2,1,0:T(1,128)S(1)}, f32[1,1,4096]{2,1,0:T(1,128)S(1)}, u32[]{:S(2)}, u32[]{:S(2)}) collective-permute-start(f32[1,1,4096]{2,1,0:T(1,128)S(1)} %get-tuple-element.40), channel_id=1, source_target_pairs={{0,1},{1,2},{2,3},{4,5},{5,6},{6,7},{8,9},{9,10},{10,11},{12,13},{... | collective-permute-start | bytes 49160 | tf_op jit(solution)/shard_map/ppermute | solution.py:21
  39.3 4.9 %collective-permute-start.11 = (f32[1,1,4096]{2,1,0:T(1,128)S(1)}, f32[1,1,4096]{2,1,0:T(1,128)S(1)}, u32[]{:S(2)}, u32[]{:S(2)}) collective-permute-start(f32[1,1,4096]{2,1,0:T(1,128)S(1)} %get-tuple-element.30), channel_id=1, source_target_pairs={{0,1},{1,2},{2,3},{4,5},{5,6},{6,7},{8,9},{9,10},{10,11},{12,13},{... | collective-permute-start | bytes 49160 | tf_op jit(solution)/shard_map/ppermute | solution.py:21
  46.5 4.9 %collective-permute-start.13 = (f32[1,1,4096]{2,1,0:T(1,128)S(1)}, f32[1,1,4096]{2,1,0:T(1,128)S(1)}, u32[]{:S(2)}, u32[]{:S(2)}) collective-permute-start(f32[1,1,4096]{2,1,0:T(1,128)S(1)} %get-tuple-element.28), channel_id=1, source_target_pairs={{0,1},{1,2},{2,3},{4,5},{5,6},{6,7},{8,9},{9,10},{10,11},{12,13},{... | collective-permute-start | bytes 49160 | tf_op jit(solution)/shard_map/ppermute | solution.py:21
  54.0 4.9 %collective-permute-start.15 = (f32[1,1,4096]{2,1,0:T(1,128)S(1)}, f32[1,1,4096]{2,1,0:T(1,128)S(1)}, u32[]{:S(2)}, u32[]{:S(2)}) collective-permute-start(f32[1,1,4096]{2,1,0:T(1,128)S(1)} %get-tuple-element.22), channel_id=1, source_target_pairs={{0,1},{1,2},{2,3},{4,5},{5,6},{6,7},{8,9},{9,10},{10,11},{12,13},{... | collective-permute-start | bytes 49160 | tf_op jit(solution)/shard_map/ppermute | solution.py:21
  60.2 2.8 %reshape.582 = f32[1,8,49152]{2,0,1:T(1,128)} reshape(f32[1,3,32,4096]{3,2,1,0:T(8,128)S(1)} %pad_maximum_fusion) | data formatting | bytes 3145728 | tf_op jit(solution)/shard_map/reshape | solution.py:76
  63.0 6.0 %all-to-all-start = ((f32[1,8,49152]{2,0,1:T(1,128)}), f32[1,8,49152]{2,0,1:T(1,128)}, u32[]{:S(2)}, u32[]{:S(2)}) async-start(f32[1,8,49152]{2,0,1:T(1,128)} %reshape.582), calls=%async_computation | async-start | bytes 3145728 | tf_op jit(solution)/shard_map/all_to_all | solution.py:77
  69.0 37.9 %all-to-all-done = f32[1,8,49152]{2,0,1:T(1,128)} async-done(((f32[1,8,49152]{2,0,1:T(1,128)}), f32[1,8,49152]{2,0,1:T(1,128)}, u32[]{:S(2)}, u32[]{:S(2)}) %all-to-all-start) | async-done | bytes 1572896 | tf_op jit(solution)/shard_map/all_to_all | solution.py:77
  106.9 2.3 %copy.18 = f32[1,8,49152]{2,1,0:T(8,128)S(1)} copy(f32[1,8,49152]{2,0,1:T(1,128)} %all-to-all-done) | data formatting | bytes 3145728
  109.2 2.1 %gather_fusion.1 = f32[8,49152]{1,0:T(8,128)} fusion(f32[8,49152]{1,0:T(8,128)S(1)} %bitcast.62, s32[1024]{0:T(1024)S(1)} %pad_clamp_fusion), kind=kCustom, calls=%fused_computation.1 | custom fusion | bytes 3145760 | tf_op jit(solution)/shard_map/jit(_take)/gather | solution.py:78
  111.3 1.6 bitcast_select_fusion
  112.9 2.8 %copy.14 = f32[8,1,49152]{2,1,0:T(1,128)} copy(f32[8,1,49152]{2,0,1:T(8,128)S(1)} %bitcast_select_fusion) | data formatting | bytes 3145728 | tf_op jit(solution)/shard_map/jit(_take)/select_n | solution.py:78
  115.6 4.3 %all-to-all-start.1 = ((f32[8,1,49152]{2,1,0:T(1,128)}), f32[8,1,49152]{2,1,0:T(1,128)S(1)}, u32[]{:S(2)}, u32[]{:S(2)}) async-start(f32[8,1,49152]{2,1,0:T(1,128)} %copy.14), calls=%async_computation.1 | async-start | bytes 3145728 | tf_op jit(solution)/shard_map/all_to_all | solution.py:79
  120.1 1.7 gather_fusion
  123.1 8.1 %psum.14 = f32[1]{0:T(128)} all-reduce(f32[1]{0:T(128)} %bitcast.13), channel_id=1, replica_groups=mesh['dom'=8,'rows'=4] {'rows'}, use_global_device_ids=true, to_apply=%region_1.2 | all-reduce | flops 1 | bytes 8 | tf_op jit(solution)/shard_map/psum | solution.py:70
  131.1 31.7 %pmax.7 = f32[]{:T(128)} all-reduce(f32[]{:T(128)} %bitcast.14), channel_id=1, replica_groups=mesh['dom'=8,'rows'=4] {'dom'}, use_global_device_ids=true, to_apply=%region_2.3 | all-reduce | flops 1 | bytes 8 | tf_op jit(solution)/shard_map/pmax | solution.py:72
  164.2 24.4 %psum.15 = f32[]{:T(128)} all-reduce(f32[]{:T(128)} %bitcast.16), channel_id=1, replica_groups=mesh['dom'=8,'rows'=4] {'dom'}, use_global_device_ids=true, to_apply=%region_3.4 | all-reduce | flops 1 | bytes 8 | tf_op jit(solution)/shard_map/psum | solution.py:73
  190.5 3.7 %reduce.2 = f32[8,49152]{1,0:T(8,128)S(1)} reduce(f32[8,1,49152]{2,1,0:T(1,128)S(1)} %all-to-all-done.1, f32[]{:T(128)} %constant.62), dimensions={1}, to_apply=%all_to_all.8.reduce_sub_computation | reduce | bytes 3145732 | tf_op jit(solution)/shard_map/all_to_all | solution.py:79
  194.2 1.6 reshape.583
  (79 shorter events, 19.9 us)
Async XLA Ops:
  2.1 5.3 %copy-start.1 = (f32[1,3,32,4096]{3,2,1,0:T(8,128)S(1)}, f32[1,3,32,4096]{3,2,1,0:T(8,128)}, u32[]{:S(2)}) copy-start(f32[1,3,32,4096]{3,2,1,0:T(8,128)} %param.6) | copy-start | bytes 4718596
  2.1 4.7 %collective-permute-start = (f32[1,1,4096]{2,1,0:T(1,128)S(1)}, f32[1,1,4096]{2,1,0:T(1,128)S(1)}, u32[]{:S(2)}, u32[]{:S(2)}) collective-permute-start(f32[1,1,4096]{2,1,0:T(1,128)S(1)} %get-tuple-element.67), channel_id=1, source_target_pairs={{1,0},{2,1},{3,2},{5,4},{6,5},{7,6},{9,8},{10,9},{11,10},{13,12},{... | collective-permute-start | bytes 49160 | tf_op jit(solution)/shard_map/ppermute | solution.py:23
  3.6 3.9 %collective-permute-start.1 = (f32[1,1,4096]{2,1,0:T(1,128)S(1)}, f32[1,1,4096]{2,1,0:T(1,128)S(1)}, u32[]{:S(2)}, u32[]{:S(2)}) collective-permute-start(f32[1,1,4096]{2,1,0:T(1,128)S(1)} %get-tuple-element.68), channel_id=1, source_target_pairs={{0,1},{1,2},{2,3},{4,5},{5,6},{6,7},{8,9},{9,10},{10,11},{12,13},{... | collective-permute-start | bytes 49160 | tf_op jit(solution)/shard_map/ppermute | solution.py:21
  7.8 6.7 %copy-start = (f32[32,4096]{1,0:T(8,128)S(1)}, f32[32,4096]{1,0:T(8,128)}, u32[]{:S(2)}) copy-start(f32[32,4096]{1,0:T(8,128)} %param.7) | copy-start | bytes 1572868
  8.0 6.9 %collective-permute-start.2 = (f32[1,1,4096]{2,1,0:T(1,128)S(1)}, f32[1,1,4096]{2,1,0:T(1,128)S(1)}, u32[]{:S(2)}, u32[]{:S(2)}) collective-permute-start(f32[1,1,4096]{2,1,0:T(1,128)S(1)} %get-tuple-element.61), channel_id=1, source_target_pairs={{1,0},{2,1},{3,2},{5,4},{6,5},{7,6},{9,8},{10,9},{11,10},{13,12},{... | collective-permute-start | bytes 49160 | tf_op jit(solution)/shard_map/ppermute | solution.py:23
  9.3 5.9 %collective-permute-start.3 = (f32[1,1,4096]{2,1,0:T(1,128)S(1)}, f32[1,1,4096]{2,1,0:T(1,128)S(1)}, u32[]{:S(2)}, u32[]{:S(2)}) collective-permute-start(f32[1,1,4096]{2,1,0:T(1,128)S(1)} %get-tuple-element.62), channel_id=1, source_target_pairs={{0,1},{1,2},{2,3},{4,5},{5,6},{6,7},{8,9},{9,10},{10,11},{12,13},{... | collective-permute-start | bytes 49160 | tf_op jit(solution)/shard_map/ppermute | solution.py:21
  15.7 6.2 %collective-permute-start.4 = (f32[1,1,4096]{2,1,0:T(1,128)S(1)}, f32[1,1,4096]{2,1,0:T(1,128)S(1)}, u32[]{:S(2)}, u32[]{:S(2)}) collective-permute-start(f32[1,1,4096]{2,1,0:T(1,128)S(1)} %get-tuple-element.59), channel_id=1, source_target_pairs={{1,0},{2,1},{3,2},{5,4},{6,5},{7,6},{9,8},{10,9},{11,10},{13,12},{... | collective-permute-start | bytes 49160 | tf_op jit(solution)/shard_map/ppermute | solution.py:23
  17.0 5.7 %collective-permute-start.5 = (f32[1,1,4096]{2,1,0:T(1,128)S(1)}, f32[1,1,4096]{2,1,0:T(1,128)S(1)}, u32[]{:S(2)}, u32[]{:S(2)}) collective-permute-start(f32[1,1,4096]{2,1,0:T(1,128)S(1)} %get-tuple-element.60), channel_id=1, source_target_pairs={{0,1},{1,2},{2,3},{4,5},{5,6},{6,7},{8,9},{9,10},{10,11},{12,13},{... | collective-permute-start | bytes 49160 | tf_op jit(solution)/shard_map/ppermute | solution.py:21
  23.2 6.6 %collective-permute-start.6 = (f32[1,1,4096]{2,1,0:T(1,128)S(1)}, f32[1,1,4096]{2,1,0:T(1,128)S(1)}, u32[]{:S(2)}, u32[]{:S(2)}) collective-permute-start(f32[1,1,4096]{2,1,0:T(1,128)S(1)} %get-tuple-element.41), channel_id=1, source_target_pairs={{1,0},{2,1},{3,2},{5,4},{6,5},{7,6},{9,8},{10,9},{11,10},{13,12},{... | collective-permute-start | bytes 49160 | tf_op jit(solution)/shard_map/ppermute | solution.py:23
  24.5 5.7 %collective-permute-start.7 = (f32[1,1,4096]{2,1,0:T(1,128)S(1)}, f32[1,1,4096]{2,1,0:T(1,128)S(1)}, u32[]{:S(2)}, u32[]{:S(2)}) collective-permute-start(f32[1,1,4096]{2,1,0:T(1,128)S(1)} %get-tuple-element.42), channel_id=1, source_target_pairs={{0,1},{1,2},{2,3},{4,5},{5,6},{6,7},{8,9},{9,10},{10,11},{12,13},{... | collective-permute-start | bytes 49160 | tf_op jit(solution)/shard_map/ppermute | solution.py:21
  30.4 6.2 %collective-permute-start.8 = (f32[1,1,4096]{2,1,0:T(1,128)S(1)}, f32[1,1,4096]{2,1,0:T(1,128)S(1)}, u32[]{:S(2)}, u32[]{:S(2)}) collective-permute-start(f32[1,1,4096]{2,1,0:T(1,128)S(1)} %get-tuple-element.39), channel_id=1, source_target_pairs={{1,0},{2,1},{3,2},{5,4},{6,5},{7,6},{9,8},{10,9},{11,10},{13,12},{... | collective-permute-start | bytes 49160 | tf_op jit(solution)/shard_map/ppermute | solution.py:23
  31.7 5.7 %collective-permute-start.9 = (f32[1,1,4096]{2,1,0:T(1,128)S(1)}, f32[1,1,4096]{2,1,0:T(1,128)S(1)}, u32[]{:S(2)}, u32[]{:S(2)}) collective-permute-start(f32[1,1,4096]{2,1,0:T(1,128)S(1)} %get-tuple-element.40), channel_id=1, source_target_pairs={{0,1},{1,2},{2,3},{4,5},{5,6},{6,7},{8,9},{9,10},{10,11},{12,13},{... | collective-permute-start | bytes 49160 | tf_op jit(solution)/shard_map/ppermute | solution.py:21
  38.0 6.6 %collective-permute-start.10 = (f32[1,1,4096]{2,1,0:T(1,128)S(1)}, f32[1,1,4096]{2,1,0:T(1,128)S(1)}, u32[]{:S(2)}, u32[]{:S(2)}) collective-permute-start(f32[1,1,4096]{2,1,0:T(1,128)S(1)} %get-tuple-element.29), channel_id=1, source_target_pairs={{1,0},{2,1},{3,2},{5,4},{6,5},{7,6},{9,8},{10,9},{11,10},{13,12},{... | collective-permute-start | bytes 49160 | tf_op jit(solution)/shard_map/ppermute | solution.py:23
  39.3 5.7 %collective-permute-start.11 = (f32[1,1,4096]{2,1,0:T(1,128)S(1)}, f32[1,1,4096]{2,1,0:T(1,128)S(1)}, u32[]{:S(2)}, u32[]{:S(2)}) collective-permute-start(f32[1,1,4096]{2,1,0:T(1,128)S(1)} %get-tuple-element.30), channel_id=1, source_target_pairs={{0,1},{1,2},{2,3},{4,5},{5,6},{6,7},{8,9},{9,10},{10,11},{12,13},{... | collective-permute-start | bytes 49160 | tf_op jit(solution)/shard_map/ppermute | solution.py:21
  45.2 6.2 %collective-permute-start.12 = (f32[1,1,4096]{2,1,0:T(1,128)S(1)}, f32[1,1,4096]{2,1,0:T(1,128)S(1)}, u32[]{:S(2)}, u32[]{:S(2)}) collective-permute-start(f32[1,1,4096]{2,1,0:T(1,128)S(1)} %get-tuple-element.27), channel_id=1, source_target_pairs={{1,0},{2,1},{3,2},{5,4},{6,5},{7,6},{9,8},{10,9},{11,10},{13,12},{... | collective-permute-start | bytes 49160 | tf_op jit(solution)/shard_map/ppermute | solution.py:23
  46.5 5.7 %collective-permute-start.13 = (f32[1,1,4096]{2,1,0:T(1,128)S(1)}, f32[1,1,4096]{2,1,0:T(1,128)S(1)}, u32[]{:S(2)}, u32[]{:S(2)}) collective-permute-start(f32[1,1,4096]{2,1,0:T(1,128)S(1)} %get-tuple-element.28), channel_id=1, source_target_pairs={{0,1},{1,2},{2,3},{4,5},{5,6},{6,7},{8,9},{9,10},{10,11},{12,13},{... | collective-permute-start | bytes 49160 | tf_op jit(solution)/shard_map/ppermute | solution.py:21
  52.7 6.2 %collective-permute-start.14 = (f32[1,1,4096]{2,1,0:T(1,128)S(1)}, f32[1,1,4096]{2,1,0:T(1,128)S(1)}, u32[]{:S(2)}, u32[]{:S(2)}) collective-permute-start(f32[1,1,4096]{2,1,0:T(1,128)S(1)} %get-tuple-element.21), channel_id=1, source_target_pairs={{1,0},{2,1},{3,2},{5,4},{6,5},{7,6},{9,8},{10,9},{11,10},{13,12},{... | collective-permute-start | bytes 49160 | tf_op jit(solution)/shard_map/ppermute | solution.py:23
  54.0 5.7 %collective-permute-start.15 = (f32[1,1,4096]{2,1,0:T(1,128)S(1)}, f32[1,1,4096]{2,1,0:T(1,128)S(1)}, u32[]{:S(2)}, u32[]{:S(2)}) collective-permute-start(f32[1,1,4096]{2,1,0:T(1,128)S(1)} %get-tuple-element.22), channel_id=1, source_target_pairs={{0,1},{1,2},{2,3},{4,5},{5,6},{6,7},{8,9},{9,10},{10,11},{12,13},{... | collective-permute-start | bytes 49160 | tf_op jit(solution)/shard_map/ppermute | solution.py:21
  63.0 6.0 %copy-start.5 = (s32[8]{0:T(128)S(1)}, s32[8]{0:T(128)}, u32[]{:S(2)}) copy-start(s32[8]{0:T(128)} %param.11) | copy-start | bytes 100
  63.0 43.9 %all-to-all-start = ((f32[1,8,49152]{2,0,1:T(1,128)}), f32[1,8,49152]{2,0,1:T(1,128)}, u32[]{:S(2)}, u32[]{:S(2)}) async-start(f32[1,8,49152]{2,0,1:T(1,128)} %reshape.582), calls=%async_computation | async-start | bytes 3145728 | tf_op jit(solution)/shard_map/all_to_all | solution.py:77
  115.6 4.3 %copy-start.2 = (s32[256]{0:T(256)S(1)}, s32[256]{0:T(256)}, u32[]{:S(2)}) copy-start(s32[256]{0:T(256)} %param.8) | copy-start | bytes 3076
  115.6 74.8 %all-to-all-start.1 = ((f32[8,1,49152]{2,1,0:T(1,128)}), f32[8,1,49152]{2,1,0:T(1,128)S(1)}, u32[]{:S(2)}, u32[]{:S(2)}) async-start(f32[8,1,49152]{2,1,0:T(1,128)} %copy.14), calls=%async_computation.1 | async-start | bytes 3145728 | tf_op jit(solution)/shard_map/all_to_all | solution.py:79
  119.9 1.9 copy-start.3
  119.9 1.9 copy-start.4
where the time goes:
time: 198 us; the launch traced here: 197 us
  blocking collectives  64.2 us (32%)
  starting transfers between devices  58 us (29%)
  waiting for transfers between devices  42.5 us (21%)
  local copies, waits for them, and re-layouts  15.8 us (8%)
  other arithmetic  10.4 us (5%)
  between operations  5.97 us (3%)
    all_to_all x1, waiting for transfers between devices, shards(): lax.all_to_all(subregion_tiles, 'dom', split_axis=1, concat_axis=0, tiled...  37.9 us
    ppermute x8, starting transfers between devices, extended(): lax.ppermute(tail, axis, [(i, (i + 1) % count) for i in range(ends)])  37.3 us
    pmax x1, blocking collectives, shards(): peak = lax.pmax(local_peak, 'dom')  31.7 us
    psum x1, blocking collectives, shards(): total = lax.psum(jnp.sum(jnp.exp(loglik - peak)), 'dom')  24.4 us
    ppermute x8, starting transfers between devices, extended(): lax.ppermute(head, axis, [((i + 1) % count, i) for i in range(ends)])  10.5 us
    psum x1, blocking collectives, shards(): loglik = lax.psum(-0.5 * jnp.sum(misfit, axis=1), 'rows')  8.06 us
    all_to_all x1, starting transfers between devices, shards(): lax.all_to_all(subregion_tiles, 'dom', split_axis=1, concat_axis=0, tiled...  5.97 us
    ppermute x8, waiting for transfers between devices, extended(): lax.ppermute(tail, axis, [(i, (i + 1) % count) for i in range(ends)])  4.65 us
  transfers between devices with their start and end apart: 18, of which 9 were waited for; matrix products, arithmetic and copies ran while one was open for 2% of the time, Pallas kernels for 0%

commit v1 on v0

v1 whole, which is shorter than its diff:
```python
import jax
import jax.numpy as jnp
from jax import lax
from jax.experimental import pallas as pl
from jax.experimental.pallas import tpu as pltpu
from jax.sharding import PartitionSpec as P

STEPS = 4
HALO = 2 * STEPS
LANES = 128

time_step = 0.5
coriolis = 0.2


def forecast_steps(h, u, v, d, top_open, bottom_open):
    n_rows, n_cols = h.shape
    for _ in range(STEPS):
        du = d * u
        dv = d * v
        dx = 0.5 * (pltpu.roll(du, n_cols - 1, 1) - pltpu.roll(du, 1, 1))
        dy = 0.5 * (pltpu.roll(dv, n_rows - 1, 0) - pltpu.roll(dv, 1, 0))
        h = h - time_step * (dx + dy)
        h = jnp.concatenate(
            [h[:HALO] * top_open, h[HALO : n_rows - HALO], h[n_rows - HALO :] * bottom_open], axis=0
        )
        dx = 0.5 * (pltpu.roll(h, n_cols - 1, 1) - pltpu.roll(h, 1, 1))
        u = u - time_step * dx + (time_step * coriolis) * v
        dy = 0.5 * (pltpu.roll(h, n_rows - 1, 0) - pltpu.roll(h, 1, 0))
        v = v - time_step * dy - (time_step * coriolis) * u
    return h, u, v


def forecast_kernel(open_ref, fields_ref, depth_ref, above_ref, below_ref, out_ref, *, width, piece):
    n_cols = fields_ref.shape[-1]
    n_rows = fields_ref.shape[-2]
    top_open = open_ref[0].astype(jnp.float32)
    bottom_open = open_ref[1].astype(jnp.float32)
    lane = lax.broadcasted_iota(jnp.int32, (n_rows + 2 * HALO, LANES), 1)

    def chunk(c, carry):
        start = pl.multiple_of(c * width, LANES)
        left = pl.multiple_of(jnp.where(c == 0, n_cols, start) - LANES, LANES)
        right = pl.multiple_of(jnp.where(start + width == n_cols, 0, start + width), LANES)

        def rows_of(k, at, size):
            mid = depth_ref[:, pl.ds(at, size)] if k == 3 else fields_ref[0, k, :, pl.ds(at, size)]
            return jnp.concatenate(
                [above_ref[k, :, pl.ds(at, size)], mid, below_ref[k, :, pl.ds(at, size)]], axis=0
            )

        def window(k):
            rim = jnp.where(lane < LANES // 2, rows_of(k, right, LANES), rows_of(k, left, LANES))
            return jnp.concatenate([rows_of(k, start, width), rim], axis=1)

        done = forecast_steps(window(0), window(1), window(2), window(3), top_open, bottom_open)
        for k in range(3):
            for q in range(width // piece):
                out_ref[c * (width // piece) + q, k] = done[k][HALO : HALO + n_rows, q * piece : (q + 1) * piece]
        return carry

    lax.fori_loop(0, n_cols // width, chunk, 0)


def forecast(fields, depth, above, below, opens, pieces):
    n_rows, n_cols = depth.shape
    piece = n_cols // pieces
    width = max(512, piece)
    vmem = pl.BlockSpec(memory_space=pltpu.VMEM)
    return pl.pallas_call(
        lambda *refs: forecast_kernel(*refs, width=width, piece=piece),
        out_shape=jax.ShapeDtypeStruct((pieces, 3, n_rows, piece), jnp.float32),
        in_specs=[pl.BlockSpec(memory_space=pltpu.SMEM), vmem, vmem, vmem, vmem],
        out_specs=vmem,
        compiler_params=pltpu.CompilerParams(vmem_limit_bytes=48 * 2**20),
        name="forecast",
    )(opens, fields, depth, above, below)


def copy_block(parents_ref, src_ref, dst_ref):
    dst_ref[...] = src_ref[...]


def pick(received, parent_lookup):
    slots = parent_lookup.shape[0]
    block = (1,) + received.shape[1:]
    return pl.pallas_call(
        copy_block,
        grid_spec=pltpu.PrefetchScalarGridSpec(
            num_scalar_prefetch=1,
            grid=(slots,),
            in_specs=[pl.BlockSpec(block, lambda i, parents: (parents[i], 0, 0, 0))],
            out_specs=pl.BlockSpec(block, lambda i, parents: (i, 0, 0, 0)),
        ),
        out_shape=jax.ShapeDtypeStruct((slots,) + received.shape[1:], received.dtype),
        name="pick",
    )(parent_lookup, received)


def place_block(src_ref, dst_ref):
    dst_ref[...] = src_ref[...]


def place(pieces):
    count, comps, n_rows, piece = pieces.shape
    block = (1, comps, n_rows, piece)
    return pl.pallas_call(
        place_block,
        grid=(count,),
        in_specs=[pl.BlockSpec(block, lambda j: (j, 0, 0, 0))],
        out_specs=pl.BlockSpec(block, lambda j: (0, 0, 0, j)),
        out_shape=jax.ShapeDtypeStruct((1, comps, n_rows, count * piece), pieces.dtype),
        name="place",
    )(pieces)


def sum_over(x, axis):
    count = lax.axis_size(axis)
    step = 1
    while step < count:
        x = x + lax.ppermute(x, axis, [(i, i ^ step) for i in range(count)])
        step *= 2
    return x


def log_weight(pieces, obs_index, obs_value, obs_var):
    count, _, n_rows, piece = pieces.shape
    n_cols = count * piece
    slab = n_rows * n_cols
    offset = obs_index - lax.axis_index("rows") * slab
    inside = (offset >= 0) & (offset < slab)
    offset = jnp.clip(offset, 0, slab - 1)
    row = offset // n_cols
    col = offset % n_cols
    values = pieces[:, 0].at[col // piece, row, col % piece].get(mode="promise_in_bounds")
    misfit = jnp.sum(jnp.where(inside, (obs_value - values) ** 2 / obs_var, 0.0))
    loglik = sum_over(-0.5 * misfit, "rows")
    slots = lax.broadcasted_iota(jnp.int32, (lax.axis_size("dom"),), 0)
    every = sum_over(jnp.where(slots == lax.axis_index("dom"), loglik, 0.0), "dom")
    peak = jnp.max(every)
    total = jnp.sum(jnp.exp(every - peak))
    return (loglik - (peak + jnp.log(total)))[None]


def shards(fields, depth, obs_index, obs_value, obs_var, parent_lookup):
    count = lax.axis_size("rows")
    pieces = lax.axis_size("dom")
    head = jnp.concatenate([fields[0, :, :HALO], depth[None, :HALO]], axis=0)
    tail = jnp.concatenate([fields[0, :, -HALO:], depth[None, -HALO:]], axis=0)
    above = lax.ppermute(tail, "rows", [(i, i + 1) for i in range(count - 1)])
    below = lax.ppermute(head, "rows", [(i + 1, i) for i in range(count - 1)])
    at = lax.axis_index("rows")
    opens = jnp.stack([at > 0, at < count - 1]).astype(jnp.int32)
    prior = forecast(fields, depth, above, below, opens, pieces)
    received = lax.all_to_all(prior, "dom", split_axis=0, concat_axis=0, tiled=True)
    log_weights = log_weight(prior, obs_index, obs_value, obs_var)
    picked = pick(received, parent_lookup)
    final = lax.all_to_all(picked, "dom", split_axis=0, concat_axis=0, tiled=True)
    return log_weights, place(final)


def solution(mesh):
    in_specs = (P("dom", None, "rows", None), P("rows", None), P(), P(), P(), P())
    out_specs = (P("dom"), P("dom", None, "rows", None))
    return jax.shard_map(shards, mesh=mesh, in_specs=in_specs, out_specs=out_specs, check_vma=False)
```

time: 198 us -> 126 us (0.64)
  starting transfers between devices: 58 us -> 18.9 us
  waiting for transfers between devices: 42.5 us -> 19 us
  blocking collectives: 64.2 us -> 41.4 us
  Pallas kernels: 0 us -> 20.5 us
  other arithmetic: 10.4 us -> 3.49 us
    all_to_all x0 -> x1, blocking collectives: none -> 41.4 us  [shards(): lax.all_to_all(prior, 'dom', split_axis=0, concat_axis=0, tiled=True)]
    all_to_all x2 -> x1, waiting for transfers between devices: 37.9 us -> 0.01 us  [shards(): lax.all_to_all(picked, 'dom', split_axis=0, concat_axis=0, tiled=True)]
    ppermute x16 -> x7, starting transfers between devices: 47.8 us -> 14.6 us  [the longest x5 10.8 us: sum_over(): x = x + lax.ppermute(x, axis, [(i, i ^ step) for i in range(count)])]
    psum x2 -> x0, blocking collectives: 32.5 us -> none  [the longest x1 24.4 us: shards(): total = lax.psum(jnp.sum(jnp.exp(loglik - peak)), 'dom')]
    pmax x1 -> x0, blocking collectives: 31.7 us -> none  [shards(): peak = lax.pmax(local_peak, 'dom')]
    pallas_call x0 -> x3, Pallas kernels: none -> 20.5 us  [the longest x1 9.01 us: forecast(): pl.pallas_call(lambda *refs: forecast_kernel(*refs, width=width, piece=pi...]
    ppermute x16 -> x7, waiting for transfers between devices: 4.67 us -> 19 us  [the longest x5 15.1 us: sum_over(): x = x + lax.ppermute(x, axis, [(i, i ^ step) for i in range(count)])]
    all_to_all x2 -> x1, starting transfers between devices: 10.2 us -> 4.33 us  [shards(): lax.all_to_all(picked, 'dom', split_axis=0, concat_axis=0, tiled=True)]
  transfers between devices with their start and end apart: 18 -> 8, of which waited for: 9 -> 6; matrix products, arithmetic and copies ran while one was open for 2% -> 10% of each run, Pallas kernels for 0% -> 0%
where the time goes in v1:
time: 126 us; the launch traced here: 125 us
  blocking collectives  41.4 us (33%)
  Pallas kernels  20.5 us (16%)
  waiting for transfers between devices  19 us (15%)
  starting transfers between devices  18.9 us (15%)
  local copies, waits for them, and re-layouts  16.6 us (13%)
  between operations  5.15 us (4%)
  other arithmetic  3.49 us (3%)
    all_to_all x1, blocking collectives, shards(): lax.all_to_all(prior, 'dom', split_axis=0, concat_axis=0, tiled=True)  41.4 us
    ppermute x5, waiting for transfers between devices, sum_over(): x = x + lax.ppermute(x, axis, [(i, i ^ step) for i in range(count)])  15.1 us
    ppermute x5, starting transfers between devices, sum_over(): x = x + lax.ppermute(x, axis, [(i, i ^ step) for i in range(count)])  10.8 us
    pallas_call x1, Pallas kernels, forecast(): pl.pallas_call(lambda *refs: forecast_kernel(*refs, width=width, piece=pi...  9.01 us
    gather x1, local copies, waits for them, and re-layouts, log_weight(): pieces[:, 0].at[col // piece, row, col % piece]  8.54 us
    pallas_call x1, Pallas kernels, pick(): pl.pallas_call(copy_block, grid_spec=pltpu.PrefetchScalarGridSpec(num_sca...  6.09 us
    unnamed x22, local copies, waits for them, and re-layouts  5.93 us
    pallas_call x1, Pallas kernels, place(): pl.pallas_call(place_block, grid=(count,), in_specs=[pl.BlockSpec(block,...  5.41 us
  transfers between devices with their start and end apart: 8, of which 6 were waited for; matrix products, arithmetic and copies ran while one was open for 10% of the time, Pallas kernels for 0%

profile of v1, /device:TPU:0, one launch (start us, length us, event | category | flops | bytes accessed | tf_op | source)
XLA Modules:
  0.0 125.1 jit_solution(5429092569198940184)
XLA Ops:
  0.6 1.2 slice_bitcast_fusion.1
  2.0 2.5 %collective-permute-start = (f32[4,8,4096]{2,1,0:T(8,128)S(1)}, f32[4,8,4096]{2,1,0:T(8,128)S(1)}, u32[]{:S(2)}, u32[]{:S(2)}) collective-permute-start(f32[4,8,4096]{2,1,0:T(8,128)S(1)} %pad_maximum_fusion), channel_id=1, source_target_pairs={{0,1},{1,2},{2,3},{4,5},{5,6},{6,7},{8,9},{9,10},{10,11},{12,13},{... | collective-permute-start | bytes 1572872 | tf_op jit(solution)/shard_map/ppermute | solution.py:150
  5.3 1.3 %collective-permute-start.1 = (f32[4,8,4096]{2,1,0:T(8,128)}, f32[4,8,4096]{2,1,0:T(8,128)S(1)}, u32[]{:S(2)}, u32[]{:S(2)}) collective-permute-start(f32[4,8,4096]{2,1,0:T(8,128)} %pad_maximum_fusion.1), channel_id=1, source_target_pairs={{1,0},{2,1},{3,2},{5,4},{6,5},{7,6},{9,8},{10,9},{11,10},{13,12},{... | collective-permute-start | bytes 1572872 | tf_op jit(solution)/shard_map/ppermute | solution.py:151
  7.5 3.9 %collective-permute-done.1.refs_4_ = f32[4,8,4096]{2,1,0:T(8,128)S(1)} collective-permute-done((f32[4,8,4096]{2,1,0:T(8,128)}, f32[4,8,4096]{2,1,0:T(8,128)S(1)}, u32[]{:S(2)}, u32[]{:S(2)}) %collective-permute-start.1) | collective-permute-done | bytes 524320 | tf_op jit(solution)/shard_map/ppermute | solution.py:151
  12.2 1.0 copy-done.2
  13.3 1.0 copy-done.4
  14.3 1.0 copy-done.6
  15.3 9.0 %forecast.1 = f32[8,3,32,512]{3,2,1,0:T(8,128)S(1)} custom-call(s32[2]{0:T(128)S(1)} %add_convert_fusion.refs_0_, f32[1,3,32,4096]{3,2,1,0:T(8,128)S(1)} %copy-done, f32[32,4096]{1,0:T(8,128)S(1)} %copy-done.2, f32[4,8,4096]{2,1,0:T(8,128)S(1)} %copy-done.4, f32[4,8,4096]{2,1,0:T(8,128)S(1)} %copy-done.6), custom_call_target="tpu_custom_call" | custom-call | tf_op jit(solution)/shard_map/forecast/pallas_call | solution.py:70
  24.4 41.4 %all_to_all.10.src_ref = f32[8,3,32,512]{3,2,1,0:T(8,128)} all-to-all(f32[8,3,32,512]{3,2,1,0:T(8,128)S(1)} %forecast.1), channel_id=1, replica_groups=mesh['dom'=8,'rows'=4] {'dom'}, dimensions={0} | all-to-all | bytes 3145728 | tf_op jit(solution)/shard_map/all_to_all | solution.py:155
  65.8 6.1 %pick.1 = f32[8,3,32,512]{3,2,1,0:T(8,128)} custom-call(s32[8]{0:T(128)} %parents_ref.1, f32[8,3,32,512]{3,2,1,0:T(8,128)} %all_to_all.10.src_ref), custom_call_target="tpu_custom_call" | custom-call | tf_op jit(solution)/shard_map/pick/pallas_call | solution.py:87
  71.8 4.3 %all-to-all-start.1 = ((f32[8,3,32,512]{3,2,1,0:T(8,128)}), f32[8,3,32,512]{3,2,1,0:T(8,128)S(1)}, u32[]{:S(2)}, u32[]{:S(2)}) async-start(f32[8,3,32,512]{3,2,1,0:T(8,128)} %pick.1), calls=%async_computation.1 | async-start | bytes 3145728 | tf_op jit(solution)/shard_map/all_to_all | solution.py:158
  77.1 8.5 %gather_fusion = f32[256]{0:T(256)S(1)} fusion(f32[8,32,512]{2,1,0:T(8,128)} %slice_bitcast_fusion, s32[256]{0:T(256)S(1)} %fusion.3), kind=kCustom, calls=%fused_computation | custom fusion | bytes 5120 | tf_op jit(solution)/shard_map/gather | solution.py:135
  86.9 0.9 collective-permute-start.2
  88.7 1.4 %collective-permute-start.3 = (f32[]{:T(128)}, f32[]{:T(128)}, u32[]{:S(2)}, u32[]{:S(2)}) collective-permute-start(f32[]{:T(128)} %add.53), channel_id=1, source_target_pairs={{0,2},{1,3},{2,0},{3,1},{4,6},{5,7},{6,4},{7,5},{8,10},{9,11},{10,... | collective-permute-start | bytes 20 | tf_op jit(solution)/shard_map/ppermute | solution.py:121
  90.1 2.2 %collective-permute-done.3 = f32[]{:T(128)} collective-permute-done((f32[]{:T(128)}, f32[]{:T(128)}, u32[]{:S(2)}, u32[]{:S(2)}) %collective-permute-start.3) | collective-permute-done | bytes 36 | tf_op jit(solution)/shard_map/ppermute | solution.py:121
  92.9 2.1 %collective-permute-start.4 = (f32[8]{0:T(128)S(1)}, f32[8]{0:T(128)S(1)}, u32[]{:S(2)}, u32[]{:S(2)}) collective-permute-start(f32[8]{0:T(128)S(1)} %compare_select_fusion.3), channel_id=1, source_target_pairs={{0,4},{4,0},{8,12},{12,8},{16,20},{20,16},{24,28},{28,24},{1,5},{5... | collective-permute-start | bytes 104 | tf_op jit(solution)/shard_map/ppermute | solution.py:121
  95.0 1.6 %collective-permute-done.4 = f32[8]{0:T(128)S(1)} collective-permute-done((f32[8]{0:T(128)S(1)}, f32[8]{0:T(128)S(1)}, u32[]{:S(2)}, u32[]{:S(2)}) %collective-permute-start.4) | collective-permute-done | bytes 64 | tf_op jit(solution)/shard_map/ppermute | solution.py:121
  96.6 2.0 %collective-permute-start.5 = (f32[8]{0:T(128)S(1)}, f32[8]{0:T(128)S(1)}, u32[]{:S(2)}, u32[]{:S(2)}) collective-permute-start(f32[8]{0:T(128)S(1)} %fusion.8), channel_id=1, source_target_pairs={{0,8},{4,12},{8,0},{12,4},{16,24},{20,28},{24,16},{28,20},{1,9},{5... | collective-permute-start | bytes 104 | tf_op jit(solution)/shard_map/ppermute | solution.py:121
  98.6 4.1 %collective-permute-done.5 = f32[8]{0:T(128)S(1)} collective-permute-done((f32[8]{0:T(128)S(1)}, f32[8]{0:T(128)S(1)}, u32[]{:S(2)}, u32[]{:S(2)}) %collective-permute-start.5) | collective-permute-done | bytes 64 | tf_op jit(solution)/shard_map/ppermute | solution.py:121
  102.7 4.5 %collective-permute-start.6 = (f32[8]{0:T(128)S(1)}, f32[8]{0:T(128)S(1)}, u32[]{:S(2)}, u32[]{:S(2)}) collective-permute-start(f32[8]{0:T(128)S(1)} %fusion.9), channel_id=1, source_target_pairs={{0,16},{4,20},{8,24},{12,28},{16,0},{20,4},{24,8},{28,12},{1,17},{... | collective-permute-start | bytes 104 | tf_op jit(solution)/shard_map/ppermute | solution.py:121
  107.1 7.0 %collective-permute-done.6 = f32[8]{0:T(128)S(1)} collective-permute-done((f32[8]{0:T(128)S(1)}, f32[8]{0:T(128)S(1)}, u32[]{:S(2)}, u32[]{:S(2)}) %collective-permute-start.6) | collective-permute-done | bytes 64 | tf_op jit(solution)/shard_map/ppermute | solution.py:121
  114.7 1.3 %exponential_reduce_fusion = f32[]{:T(128)} fusion(f32[8]{0:T(128)S(1)} %get-tuple-element.3, f32[]{:T(128)} %get-tuple-element.2), kind=kLoop, calls=%fused_computation.32 | loop fusion | flops 15 | bytes 40 | tf_op jit(solution)/shard_map/reduce_sum | solution.py:141
  117.4 1.2 copy-done.7
  118.5 5.4 %place.1 = f32[1,3,32,4096]{3,2,1,0:T(8,128)} custom-call(f32[8,3,32,512]{3,2,1,0:T(8,128)} %copy-done.7), custom_call_target="tpu_custom_call" | custom-call | tf_op jit(solution)/shard_map/place/pallas_call | solution.py:107
  (32 shorter events, 5.0 us)
Async XLA Ops:
  0.6 1.3 %copy-start.1 = (f32[32,4096]{1,0:T(8,128)S(1)}, f32[32,4096]{1,0:T(8,128)}, u32[]{:S(2)}) copy-start(f32[32,4096]{1,0:T(8,128)} %refs_2_.1) | copy-start | bytes 1572868
  1.9 10.3 %copy-start = (f32[1,3,32,4096]{3,2,1,0:T(8,128)S(1)}, f32[1,3,32,4096]{3,2,1,0:T(8,128)}, u32[]{:S(2)}) copy-start(f32[1,3,32,4096]{3,2,1,0:T(8,128)} %refs_1_.1) | copy-start | bytes 4718596
  2.0 4.7 %collective-permute-start = (f32[4,8,4096]{2,1,0:T(8,128)S(1)}, f32[4,8,4096]{2,1,0:T(8,128)S(1)}, u32[]{:S(2)}, u32[]{:S(2)}) collective-permute-start(f32[4,8,4096]{2,1,0:T(8,128)S(1)} %pad_maximum_fusion), channel_id=1, source_target_pairs={{0,1},{1,2},{2,3},{4,5},{5,6},{6,7},{8,9},{9,10},{10,11},{12,13},{... | collective-permute-start | bytes 1572872 | tf_op jit(solution)/shard_map/ppermute | solution.py:150
  5.3 6.1 %collective-permute-start.1 = (f32[4,8,4096]{2,1,0:T(8,128)}, f32[4,8,4096]{2,1,0:T(8,128)S(1)}, u32[]{:S(2)}, u32[]{:S(2)}) collective-permute-start(f32[4,8,4096]{2,1,0:T(8,128)} %pad_maximum_fusion.1), channel_id=1, source_target_pairs={{1,0},{2,1},{3,2},{5,4},{6,5},{7,6},{9,8},{10,9},{11,10},{13,12},{... | collective-permute-start | bytes 1572872 | tf_op jit(solution)/shard_map/ppermute | solution.py:151
  6.7 0.8 copy-start.3
  11.4 0.8 copy-start.5
  12.2 1.0 copy-start.2
  13.3 1.0 copy-start.4
  14.3 1.0 copy-start.6
  71.8 4.4 %copy-start.8 = (s32[256]{0:T(256)S(1)}, s32[256]{0:T(256)}, u32[]{:S(2)}) copy-start(s32[256]{0:T(256)} %param.8) | copy-start | bytes 3076
  71.8 45.5 %all-to-all-start.1 = ((f32[8,3,32,512]{3,2,1,0:T(8,128)}), f32[8,3,32,512]{3,2,1,0:T(8,128)S(1)}, u32[]{:S(2)}, u32[]{:S(2)}) async-start(f32[8,3,32,512]{3,2,1,0:T(8,128)} %pick.1), calls=%async_computation.1 | async-start | bytes 3145728 | tf_op jit(solution)/shard_map/all_to_all | solution.py:158
  76.2 9.5 %copy-start.9 = (f32[256]{0:T(256)S(1)}, f32[256]{0:T(256)}, u32[]{:S(2)}) copy-start(f32[256]{0:T(256)} %param.10) | copy-start | bytes 3076
  76.2 9.5 %copy-start.10 = (f32[256]{0:T(256)S(1)}, f32[256]{0:T(256)}, u32[]{:S(2)}) copy-start(f32[256]{0:T(256)} %param.9) | copy-start | bytes 3076
  86.9 1.2 collective-permute-start.2
  88.7 3.6 %collective-permute-start.3 = (f32[]{:T(128)}, f32[]{:T(128)}, u32[]{:S(2)}, u32[]{:S(2)}) collective-permute-start(f32[]{:T(128)} %add.53), channel_id=1, source_target_pairs={{0,2},{1,3},{2,0},{3,1},{4,6},{5,7},{6,4},{7,5},{8,10},{9,11},{10,... | collective-permute-start | bytes 20 | tf_op jit(solution)/shard_map/ppermute | solution.py:121
  92.9 3.7 %collective-permute-start.4 = (f32[8]{0:T(128)S(1)}, f32[8]{0:T(128)S(1)}, u32[]{:S(2)}, u32[]{:S(2)}) collective-permute-start(f32[8]{0:T(128)S(1)} %compare_select_fusion.3), channel_id=1, source_target_pairs={{0,4},{4,0},{8,12},{12,8},{16,20},{20,16},{24,28},{28,24},{1,5},{5... | collective-permute-start | bytes 104 | tf_op jit(solution)/shard_map/ppermute | solution.py:121
  96.6 6.1 %collective-permute-start.5 = (f32[8]{0:T(128)S(1)}, f32[8]{0:T(128)S(1)}, u32[]{:S(2)}, u32[]{:S(2)}) collective-permute-start(f32[8]{0:T(128)S(1)} %fusion.8), channel_id=1, source_target_pairs={{0,8},{4,12},{8,0},{12,4},{16,24},{20,28},{24,16},{28,20},{1,9},{5... | collective-permute-start | bytes 104 | tf_op jit(solution)/shard_map/ppermute | solution.py:121
  102.7 11.5 %collective-permute-start.6 = (f32[8]{0:T(128)S(1)}, f32[8]{0:T(128)S(1)}, u32[]{:S(2)}, u32[]{:S(2)}) collective-permute-start(f32[8]{0:T(128)S(1)} %fusion.9), channel_id=1, source_target_pairs={{0,16},{4,20},{8,24},{12,28},{16,0},{20,4},{24,8},{28,12},{1,17},{... | collective-permute-start | bytes 104 | tf_op jit(solution)/shard_map/ppermute | solution.py:121
  117.4 1.2 copy-start.7
